TPU v7x, 512 devices: a whole 4x4x16 slice. The times are simulated.
512 devices in a mesh: group: 16 (over y, z_hi), seq: 32 (over x, z_lo, core).
Axes of the slice: x: 4, y: 4, z: 16 (z_hi: 4, z_lo: 4; z = z_hi * 4 + z_lo), core: 2. Of those that a mesh axis runs over, the one named last changes fastest.
Arguments:
- features: bfloat16 [65536, 768], P(('group', 'seq')), may hold values from -6 to 6
- tiles: bfloat16 [65536, 1024], P(('group', 'seq')), may hold values from -0.5 to 0.5
- tile_src: int32 [512, 8], P(('group', 'seq')), may hold values from 0 to 15
- tile_count: int32 [512], P(('group', 'seq')), may hold values from 1 to 8, as said below
- node_bucket: int32 [65536], P(('group', 'seq')), may hold values from 0 to 15
- w_qk: bfloat16 [768, 1536], replicated, may hold values from -0.3125 to 0.3125
- w_v: bfloat16 [768, 768], replicated, may hold values from -1.25 to 1.25
- bias_table: float32 [32, 256], replicated, may hold values from -2 to 300
Outputs:
- attended: bfloat16 [65536, 768], P(('group', 'seq'))
Inputs may be any that keep to these rules, and one draw needn't show every extreme that they name: `tile_count`: some row block uses all 8 slots.
All inputs are finite; a program needn't handle non-finite values.
Results may differ from a plain program's by a relative error of at most 0.012.
Values may be sent and summed in bfloat16 or wider, within the bound.
A program may use at most 64 MiB of HBM per device.

v0:
```python
import math
import jax
import jax.numpy as jnp
from jax import lax
from jax.sharding import PartitionSpec as P

H = 32
HD = 24
NB = 16
TILES = 8


def on_device(features, tiles, tile_src, tile_count, node_bucket, w_qk, w_v, bias_table):
    row_count, feat_width = features.shape
    group_count = lax.axis_size("group")
    live_flag = jnp.arange(TILES) < tile_count[0]
    tile_rows = tiles.reshape(row_count, TILES, row_count)
    sources = tile_src[0]
    gathered = lax.all_gather(features, "group", axis=0, tiled=True)
    chosen = gathered.reshape(group_count, row_count, feat_width)[sources]
    masked = tile_rows * live_flag.astype(jnp.bfloat16)[None, :, None]
    aggregated = features.astype(jnp.float32) + jnp.einsum(
        "rtc,tcd->rd", masked, chosen, preferred_element_type=jnp.float32
    )
    mean_square = jnp.mean(aggregated * aggregated, axis=-1, keepdims=True)
    normed = (aggregated * lax.rsqrt(mean_square + 1e-06)).astype(jnp.bfloat16)
    query_key = jnp.dot(normed, w_qk, preferred_element_type=jnp.float32).astype(jnp.bfloat16)
    values = jnp.dot(normed, w_v, preferred_element_type=jnp.float32).astype(jnp.bfloat16)
    bias_cube = bias_table.reshape(H, NB, NB)
    scale = 1.0 / math.sqrt(HD)
    iota_nb = jnp.arange(NB)
    queries = query_key[:, :feat_width].reshape(row_count, H, HD)
    keys_own = query_key[:, feat_width:]
    query_bias = bias_cube[:, node_bucket, :]
    start_state = (
        jnp.full((H, row_count), -1e30, jnp.float32),
        jnp.zeros((H, row_count), jnp.float32),
        jnp.zeros((H, row_count, HD), jnp.float32),
    )
    key_rows = lax.all_gather(keys_own, "seq", axis=0, tiled=True)
    value_rows = lax.all_gather(values, "seq", axis=0, tiled=True)
    bucket_rows = lax.all_gather(node_bucket, "seq", axis=0, tiled=True)
    key_total = key_rows.shape[0]
    key_block = math.gcd(key_total, 512)

    def one_block(block_index, state_in):
        peak_old, total_old, accum_old = state_in
        offset = block_index * key_block
        key_part = lax.dynamic_slice_in_dim(key_rows, offset, key_block, 0).reshape(
            key_block, H, HD
        )
        value_part = lax.dynamic_slice_in_dim(value_rows, offset, key_block, 0).reshape(
            key_block, H, HD
        )
        bucket_part = lax.dynamic_slice_in_dim(bucket_rows, offset, key_block, 0)
        onehot = (bucket_part[:, None] == iota_nb[None, :]).astype(jnp.float32)
        scores = (
            jnp.einsum("rhd,nhd->hrn", queries, key_part, preferred_element_type=jnp.float32)
            * scale
        )
        scores = scores + jnp.einsum(
            "hrb,nb->hrn", query_bias, onehot, precision=lax.Precision.HIGHEST
        )
        peak_new = jnp.maximum(peak_old, jnp.max(scores, axis=-1))
        factor = jnp.exp(peak_old - peak_new)
        weights = jnp.exp(scores - peak_new[..., None])
        total_new = total_old * factor + jnp.sum(weights, axis=-1)
        accum_new = accum_old * factor[..., None] + jnp.einsum(
            "hrn,nhd->hrd",
            weights.astype(jnp.bfloat16),
            value_part,
            preferred_element_type=jnp.float32,
        )
        return (peak_new, total_new, accum_new)

    peak_end, total_end, accum_end = lax.fori_loop(
        0, key_total // key_block, one_block, start_state
    )
    heads_out = accum_end / total_end[..., None]
    attended = heads_out.transpose(1, 0, 2).reshape(row_count, feat_width).astype(jnp.bfloat16)
    return attended


def solution(mesh):
    in_specs = (
        P(("group", "seq"), None),
        P(("group", "seq"), None),
        P(("group", "seq"), None),
        P(("group", "seq")),
        P(("group", "seq")),
        P(),
        P(),
        P(),
    )
    out_specs = P(("group", "seq"), None)
    return jax.shard_map(
        on_device, mesh=mesh, in_specs=in_specs, out_specs=out_specs, check_vma=False
    )
```

profile of v0, /device:TPU:1, one launch (start us, length us, event | category | flops | bytes accessed | tf_op | source)
XLA Modules:
  0.0 412.8 jit_solution(12334973029780764622)
XLA Ops:
  8.6 121.5 %all-gather.5.cloned.1.call-done = bf16[2048,768]{1,0:T(8,128)(2,1)} async-done(((bf16[128,768]{1,0:T(8,128)(2,1)}), bf16[2048,768]{1,0:T(8,128)(2,1)}) %all-gather.5.cloned.1.call-update) | async-done | bytes 3145744 | tf_op jit(solution)/shard_map/all_gather | solution.py:19
  130.1 3.7 gather_fusion
  133.8 2.0 multiply_reduce_fusion
  137.1 2.3 convolution_convert_fusion.1
  139.6 1.8 gather_fusion.1
  141.4 2.4 copy.28
  143.7 39.3 %all-gather = s32[32,1,128]{2,1,0:T(1,128)S(1)} all-gather(s32[1,1,128]{2,1,0:T(1,128)S(1)} %bitcast.66), channel_id=1, replica_groups=mesh['group'=16,'seq'=32] {'seq'}, dimensions={0}, use_global_device_ids=true | all-gather | bytes 16896 | tf_op jit(solution)/shard_map/all_gather | solution.py:42
  183.9 19.7 %all-gather.7.cloned.1.call-done = bf16[4096,768]{1,0:T(8,128)(2,1)} async-done(((bf16[128,768]{1,0:T(8,128)(2,1)}), bf16[4096,768]{1,0:T(8,128)(2,1)}) %all-gather.7.cloned.1.call-update) | async-done | bytes 6291472 | tf_op jit(solution)/shard_map/all_gather | solution.py:40
  203.6 71.9 %all-gather.9.cloned.1.call-done = bf16[4096,768]{1,0:T(8,128)(2,1)} async-done(((bf16[128,768]{1,0:T(8,128)(2,1)}), bf16[4096,768]{1,0:T(8,128)(2,1)}) %all-gather.9.cloned.1.call-update) | async-done | bytes 6291472 | tf_op jit(solution)/shard_map/all_gather | solution.py:41
  275.5 129.1 %while.18 = (s32[]{:T(128)}, f32[32,128]{1,0:T(8,128)S(1)}, f32[32,128]{1,0:T(8,128)}, f32[32,128,24]{1,2,0:T(8,128)S(1)}, bf16[4096,768]{1,0:T(8,128)(2,1)}, /*...) while((s32[]{:T(128)}, f32[32,128]{1,0:T(8,128)S(1)}, ...), condition=%wide.region_4.0_spmd.clone, body=%wide.region_1.0_spmd.clone.sunk | while | flops 618983424 | bytes 55515500 | solution.py:76
  276.2 2.7 constant_dynamic-slice_fusion.3
  278.9 1.4 copy.43
  280.3 2.4 copy.44
  282.7 4.5 %fusion.46 = f32[512,32,128]{2,0,1:T(8,128)S(1)} fusion(f32[32,128,16]{1,2,0:T(8,128)} %get-tuple-element.364, s32[512]{0:T(512)} %dynamic_slice.29), kind=kOutput, calls=%fused_computation.13.clone.1 | convolution fusion | flops 402661376 | bytes 8652800 | tf_op jit(solution)/shard_map/while/body/eval_jaxpr/hrb,nb->hrn/dot_general | solution.py:61
  287.2 1.8 fusion.47
  289.1 1.3 fusion.48
  290.4 1.2 fusion.50
  292.4 2.7 constant_dynamic-slice_fusion.3
  295.0 1.4 copy.43
  296.4 2.4 copy.44
  298.8 4.5 %fusion.46 = f32[512,32,128]{2,0,1:T(8,128)S(1)} fusion(f32[32,128,16]{1,2,0:T(8,128)} %get-tuple-element.364, s32[512]{0:T(512)} %dynamic_slice.29), kind=kOutput, calls=%fused_computation.13.clone.1 | convolution fusion | flops 402661376 | bytes 8652800 | tf_op jit(solution)/shard_map/while/body/eval_jaxpr/hrb,nb->hrn/dot_general | solution.py:61
  303.3 1.8 fusion.47
  305.2 1.3 fusion.48
  306.5 1.2 fusion.50
  308.5 2.7 constant_dynamic-slice_fusion.3
  311.2 1.4 copy.43
  312.6 2.4 copy.44
  314.9 4.5 %fusion.46 = f32[512,32,128]{2,0,1:T(8,128)S(1)} fusion(f32[32,128,16]{1,2,0:T(8,128)} %get-tuple-element.364, s32[512]{0:T(512)} %dynamic_slice.29), kind=kOutput, calls=%fused_computation.13.clone.1 | convolution fusion | flops 402661376 | bytes 8652800 | tf_op jit(solution)/shard_map/while/body/eval_jaxpr/hrb,nb->hrn/dot_general | solution.py:61
  319.5 1.8 fusion.47
  321.4 1.3 fusion.48
  322.7 1.2 fusion.50
  324.6 2.7 constant_dynamic-slice_fusion.3
  327.3 1.4 copy.43
  328.7 2.4 copy.44
  331.1 4.5 %fusion.46 = f32[512,32,128]{2,0,1:T(8,128)S(1)} fusion(f32[32,128,16]{1,2,0:T(8,128)} %get-tuple-element.364, s32[512]{0:T(512)} %dynamic_slice.29), kind=kOutput, calls=%fused_computation.13.clone.1 | convolution fusion | flops 402661376 | bytes 8652800 | tf_op jit(solution)/shard_map/while/body/eval_jaxpr/hrb,nb->hrn/dot_general | solution.py:61
  335.6 1.8 fusion.47
  337.5 1.3 fusion.48
  340.8 2.7 constant_dynamic-slice_fusion.3
  343.4 1.4 copy.43
  344.9 2.4 copy.44
  347.2 4.5 %fusion.46 = f32[512,32,128]{2,0,1:T(8,128)S(1)} fusion(f32[32,128,16]{1,2,0:T(8,128)} %get-tuple-element.364, s32[512]{0:T(512)} %dynamic_slice.29), kind=kOutput, calls=%fused_computation.13.clone.1 | convolution fusion | flops 402661376 | bytes 8652800 | tf_op jit(solution)/shard_map/while/body/eval_jaxpr/hrb,nb->hrn/dot_general | solution.py:61
  351.8 1.8 fusion.47
  353.6 1.3 fusion.48
  356.9 2.7 constant_dynamic-slice_fusion.3
  359.6 1.4 copy.43
  361.0 2.4 copy.44
  363.4 4.5 %fusion.46 = f32[512,32,128]{2,0,1:T(8,128)S(1)} fusion(f32[32,128,16]{1,2,0:T(8,128)} %get-tuple-element.364, s32[512]{0:T(512)} %dynamic_slice.29), kind=kOutput, calls=%fused_computation.13.clone.1 | convolution fusion | flops 402661376 | bytes 8652800 | tf_op jit(solution)/shard_map/while/body/eval_jaxpr/hrb,nb->hrn/dot_general | solution.py:61
  367.9 1.8 fusion.47
  369.8 1.3 fusion.48
  371.1 1.2 fusion.50
  373.1 2.7 constant_dynamic-slice_fusion.3
  375.7 1.4 copy.43
  377.1 2.4 copy.44
  379.5 4.5 %fusion.46 = f32[512,32,128]{2,0,1:T(8,128)S(1)} fusion(f32[32,128,16]{1,2,0:T(8,128)} %get-tuple-element.364, s32[512]{0:T(512)} %dynamic_slice.29), kind=kOutput, calls=%fused_computation.13.clone.1 | convolution fusion | flops 402661376 | bytes 8652800 | tf_op jit(solution)/shard_map/while/body/eval_jaxpr/hrb,nb->hrn/dot_general | solution.py:61
  384.0 1.8 fusion.47
  385.9 1.3 fusion.48
  387.3 1.2 fusion.50
  389.2 2.7 constant_dynamic-slice_fusion.3
  391.9 1.4 copy.43
  393.3 2.4 copy.44
  395.7 4.5 %fusion.46 = f32[512,32,128]{2,0,1:T(8,128)S(1)} fusion(f32[32,128,16]{1,2,0:T(8,128)} %get-tuple-element.364, s32[512]{0:T(512)} %dynamic_slice.29), kind=kOutput, calls=%fused_computation.13.clone.1 | convolution fusion | flops 402661376 | bytes 8652800 | tf_op jit(solution)/shard_map/while/body/eval_jaxpr/hrb,nb->hrn/dot_general | solution.py:61
  400.2 1.8 fusion.47
  402.1 1.3 fusion.48
  403.4 1.2 fusion.50
  (157 shorter events, 13.4 us)
Async XLA Ops:
  6.5 129.2 %copy-start = (bf16[768,1536]{1,0:T(8,128)(2,1)S(1)}, bf16[768,1536]{1,0:T(8,128)(2,1)}, u32[]{:S(2)}) copy-start(bf16[768,1536]{1,0:T(8,128)(2,1)} %param.15) | copy-start | bytes 7077892
  6.5 132.9 %copy-start.7 = (f32[32,256]{1,0:T(8,128)S(1)}, f32[32,256]{1,0:T(8,128)}, u32[]{:S(2)}) copy-start(f32[32,256]{1,0:T(8,128)} %param.17) | copy-start | bytes 98308
  6.5 133.0 %copy-start.8 = (s32[128]{0:T(128)S(1)}, s32[128]{0:T(128)}, u32[]{:S(2)}) copy-start(s32[128]{0:T(128)} %param.14) | copy-start | bytes 1540
  6.5 123.5 %all-gather.5.cloned.1.call-start = ((), (), s32[]{:S(2)}) async-start(), calls=%async_computation | async-start | bytes 3342336 | tf_op jit(solution)/shard_map/all_gather | solution.py:19
  7.3 196.3 %all-gather.7.cloned.1.call-start = ((), (), s32[]{:S(2)}) async-start(), calls=%async_computation.1 | async-start | bytes 6488064 | tf_op jit(solution)/shard_map/all_gather | solution.py:40
  137.0 138.5 %all-gather.9.cloned.1.call-start = ((), (), s32[]{:S(2)}) async-start(), calls=%async_computation.2 | async-start | bytes 6488064 | tf_op jit(solution)/shard_map/all_gather | solution.py:41
  275.5 3.3 copy-start.5
  282.7 4.5 %copy-start.2 = (bf16[128,32,24]{0,2,1:T(8,128)(2,1)S(1)}, bf16[128,32,24]{0,2,1:T(8,128)(2,1)}, u32[]{:S(2)}) copy-start(bf16[128,32,24]{0,2,1:T(8,128)(2,1)} %get-tuple-element.362) | copy-start | bytes 589828 | tf_op jit(solution)/shard_map/while
  289.0 1.3 copy-start.3
  289.0 1.3 copy-start.1
  290.4 1.3 copy-start.6
  290.4 1.3 copy-start.4
  291.7 3.4 copy-start.5
  298.8 4.5 %copy-start.2 = (bf16[128,32,24]{0,2,1:T(8,128)(2,1)S(1)}, bf16[128,32,24]{0,2,1:T(8,128)(2,1)}, u32[]{:S(2)}) copy-start(bf16[128,32,24]{0,2,1:T(8,128)(2,1)} %get-tuple-element.362) | copy-start | bytes 589828 | tf_op jit(solution)/shard_map/while
  305.2 1.3 copy-start.3
  305.2 1.3 copy-start.1
  306.5 1.3 copy-start.6
  306.5 1.3 copy-start.4
  307.8 3.4 copy-start.5
  314.9 4.5 %copy-start.2 = (bf16[128,32,24]{0,2,1:T(8,128)(2,1)S(1)}, bf16[128,32,24]{0,2,1:T(8,128)(2,1)}, u32[]{:S(2)}) copy-start(bf16[128,32,24]{0,2,1:T(8,128)(2,1)} %get-tuple-element.362) | copy-start | bytes 589828 | tf_op jit(solution)/shard_map/while
  321.3 1.3 copy-start.3
  321.3 1.3 copy-start.1
  322.6 1.3 copy-start.6
  322.7 1.3 copy-start.4
  324.0 3.4 copy-start.5
  331.1 4.5 %copy-start.2 = (bf16[128,32,24]{0,2,1:T(8,128)(2,1)S(1)}, bf16[128,32,24]{0,2,1:T(8,128)(2,1)}, u32[]{:S(2)}) copy-start(bf16[128,32,24]{0,2,1:T(8,128)(2,1)} %get-tuple-element.362) | copy-start | bytes 589828 | tf_op jit(solution)/shard_map/while
  337.5 1.3 copy-start.3
  337.5 1.3 copy-start.1
  338.8 1.3 copy-start.6
  338.8 1.3 copy-start.4
  340.1 3.4 copy-start.5
  347.2 4.5 %copy-start.2 = (bf16[128,32,24]{0,2,1:T(8,128)(2,1)S(1)}, bf16[128,32,24]{0,2,1:T(8,128)(2,1)}, u32[]{:S(2)}) copy-start(bf16[128,32,24]{0,2,1:T(8,128)(2,1)} %get-tuple-element.362) | copy-start | bytes 589828 | tf_op jit(solution)/shard_map/while
  353.6 1.3 copy-start.3
  353.6 1.3 copy-start.1
  354.9 1.3 copy-start.6
  355.0 1.3 copy-start.4
  356.2 3.4 copy-start.5
  363.4 4.5 %copy-start.2 = (bf16[128,32,24]{0,2,1:T(8,128)(2,1)S(1)}, bf16[128,32,24]{0,2,1:T(8,128)(2,1)}, u32[]{:S(2)}) copy-start(bf16[128,32,24]{0,2,1:T(8,128)(2,1)} %get-tuple-element.362) | copy-start | bytes 589828 | tf_op jit(solution)/shard_map/while
  369.8 1.3 copy-start.3
  369.8 1.3 copy-start.1
  371.1 1.3 copy-start.6
  371.1 1.3 copy-start.4
  372.4 3.4 copy-start.5
  379.5 4.5 %copy-start.2 = (bf16[128,32,24]{0,2,1:T(8,128)(2,1)S(1)}, bf16[128,32,24]{0,2,1:T(8,128)(2,1)}, u32[]{:S(2)}) copy-start(bf16[128,32,24]{0,2,1:T(8,128)(2,1)} %get-tuple-element.362) | copy-start | bytes 589828 | tf_op jit(solution)/shard_map/while
  385.9 1.3 copy-start.3
  385.9 1.3 copy-start.1
  387.2 1.3 copy-start.6
  387.2 1.3 copy-start.4
  388.5 3.4 copy-start.5
  395.7 4.5 %copy-start.2 = (bf16[128,32,24]{0,2,1:T(8,128)(2,1)S(1)}, bf16[128,32,24]{0,2,1:T(8,128)(2,1)}, u32[]{:S(2)}) copy-start(bf16[128,32,24]{0,2,1:T(8,128)(2,1)} %get-tuple-element.362) | copy-start | bytes 589828 | tf_op jit(solution)/shard_map/while
  402.0 1.3 copy-start.3
  402.0 1.3 copy-start.1
  403.3 1.3 copy-start.6
  403.4 1.3 copy-start.4
Sparse Core Ops, SparseCore 0:
  10.4 119.6 all-gather.4
  137.1 66.4 all-gather.6
  205.8 69.7 all-gather.8
where the time goes:
time: 414 us; the launch traced here: 413 us
  waiting for transfers between devices  214 us (52%)
  local copies, waits for them, and re-layouts  67.4 us (16%)
  matrix products  65.4 us (16%)
  blocking collectives  39.3 us (9%)
  between operations  13.9 us (3%)
  other arithmetic  11.7 us (3%)
    all_gather x1, waiting for transfers between devices, on_device(): gathered = lax.all_gather(features, 'group', axis=0, tiled=True)  121 us
    all_gather x1, waiting for transfers between devices, on_device(): value_rows = lax.all_gather(values, 'seq', axis=0, tiled=True)  71.9 us
    dynamic_slice x16, local copies, waits for them, and re-layouts, one_block(): lax.dynamic_slice_in_dim(value_rows, offset, key_block, 0)  40.3 us
    all_gather x1, blocking collectives, on_device(): bucket_rows = lax.all_gather(node_bucket, 'seq', axis=0, tiled=True)  39.3 us
    dot_general x8, matrix products, one_block(): jnp.einsum('hrb,nb->hrn', query_bias, onehot, precision=lax.Precision.HIG...  36.1 us
    all_gather x1, waiting for transfers between devices, on_device(): key_rows = lax.all_gather(keys_own, 'seq', axis=0, tiled=True)  19.7 us
    dot_general x8, matrix products, one_block(): jnp.einsum('rhd,nhd->hrn', queries, key_part, preferred_element_type=jnp....  14.7 us
    dynamic_slice x8, local copies, waits for them, and re-layouts, one_block(): lax.dynamic_slice_in_dim(key_rows, offset, key_block, 0)  11.3 us
  transfers between devices with their start and end apart: 3, of which 3 were waited for; matrix products, arithmetic and copies ran while one was open for 2% of the time, Pallas kernels for 0%

commit v1 on v0

--- a/solution.py
+++ b/solution.py
@@ -16,7 +16,9 @@
     live_flag = jnp.arange(TILES) < tile_count[0]
     tile_rows = tiles.reshape(row_count, TILES, row_count)
     sources = tile_src[0]
-    gathered = lax.all_gather(features, "group", axis=0, tiled=True)
+    gathered = jnp.concatenate(
+        lax.all_to_all(jnp.stack([features] * lax.axis_size("group")), "group", 0, 0), axis=0
+    )
     chosen = gathered.reshape(group_count, row_count, feat_width)[sources]
     masked = tile_rows * live_flag.astype(jnp.bfloat16)[None, :, None]
     aggregated = features.astype(jnp.float32) + jnp.einsum(

time: 414 us -> 457 us (1.10)
  starting transfers between devices: 0.08 us -> 18.6 us
  waiting for transfers between devices: 214 us -> 230 us
  blocking collectives: 39.3 us -> 44.7 us
    all_to_all x0 -> x1, waiting for transfers between devices: none -> 140 us  [on_device(): lax.all_to_all(jnp.stack([features] * lax.axis_size('group')), 'group', 0...]
    all_gather x1 -> x0, waiting for transfers between devices: 121 us -> none  [on_device(): gathered = lax.all_gather(features, 'group', axis=0, tiled=True)]
    all_to_all x0 -> x1, starting transfers between devices: none -> 18.5 us  [on_device(): lax.all_to_all(jnp.stack([features] * lax.axis_size('group')), 'group', 0...]
    all_gather x1, blocking collectives: 39.3 us -> 44.7 us  [on_device(): bucket_rows = lax.all_gather(node_bucket, 'seq', axis=0, tiled=True)]
where the time goes in v1:
time: 457 us; the launch traced here: 456 us
  waiting for transfers between devices  230 us (50%)
  local copies, waits for them, and re-layouts  70.4 us (15%)
  matrix products  65.3 us (14%)
  blocking collectives  44.7 us (10%)
  starting transfers between devices  18.6 us (4%)
  between operations  14.2 us (3%)
  other arithmetic  11 us (2%)
    all_to_all x1, waiting for transfers between devices, on_device(): lax.all_to_all(jnp.stack([features] * lax.axis_size('group')), 'group', 0...  140 us
    all_gather x1, waiting for transfers between devices, on_device(): value_rows = lax.all_gather(values, 'seq', axis=0, tiled=True)  71.8 us
    all_gather x1, blocking collectives, on_device(): bucket_rows = lax.all_gather(node_bucket, 'seq', axis=0, tiled=True)  44.7 us
    dynamic_slice x16, local copies, waits for them, and re-layouts, one_block(): lax.dynamic_slice_in_dim(value_rows, offset, key_block, 0)  40.1 us
    dot_general x8, matrix products, one_block(): jnp.einsum('hrb,nb->hrn', query_bias, onehot, precision=lax.Precision.HIG...  36.1 us
    all_to_all x1, starting transfers between devices, on_device(): lax.all_to_all(jnp.stack([features] * lax.axis_size('group')), 'group', 0...  18.5 us
    all_gather x1, waiting for transfers between devices, on_device(): key_rows = lax.all_gather(keys_own, 'seq', axis=0, tiled=True)  18.3 us
    dot_general x8, matrix products, one_block(): jnp.einsum('rhd,nhd->hrn', queries, key_part, preferred_element_type=jnp....  14.7 us
  transfers between devices with their start and end apart: 3, of which 3 were waited for; matrix products, arithmetic and copies ran while one was open for 2% of the time, Pallas kernels for 0%

profile of v1, /device:TPU:1, one launch (start us, length us, event | category | flops | bytes accessed | tf_op | source)
XLA Modules:
  0.0 455.7 jit_solution(7229768738576481999)
XLA Ops:
  6.5 3.1 stack.2
  9.6 18.5 %all-to-all-start = ((bf16[16,128,768]{2,1,0:T(8,128)(2,1)}), bf16[16,128,768]{2,1,0:T(8,128)(2,1)}, u32[]{:S(2)}, u32[]{:S(2)}) async-start(bf16[16,128,768]{2,1,0:T(8,128)(2,1)} %stack.2), calls=%async_computation | async-start | bytes 6291456 | tf_op jit(solution)/shard_map/all_to_all | solution.py:20
  28.9 140.3 %all-to-all-done = bf16[16,128,768]{2,1,0:T(8,128)(2,1)} async-done(((bf16[16,128,768]{2,1,0:T(8,128)(2,1)}), bf16[16,128,768]{2,1,0:T(8,128)(2,1)}, u32[]{:S(2)}, u32[]{:S(2)}) %all-to-all-start) | async-done | bytes 3145760 | tf_op jit(solution)/shard_map/all_to_all | solution.py:20
  169.2 3.7 gather_fusion
  172.9 1.9 multiply_reduce_fusion
  176.1 2.3 convolution_convert_fusion.1
  178.6 1.8 gather_fusion.1
  180.4 2.4 copy.28
  182.8 44.7 %all-gather = s32[32,1,128]{2,1,0:T(1,128)S(1)} all-gather(s32[1,1,128]{2,1,0:T(1,128)S(1)} %bitcast.64), channel_id=1, replica_groups=mesh['group'=16,'seq'=32] {'seq'}, dimensions={0}, use_global_device_ids=true | all-gather | bytes 16896 | tf_op jit(solution)/shard_map/all_gather | solution.py:44
  228.3 18.3 %all-gather.4.cloned.1.call-done = bf16[4096,768]{1,0:T(8,128)(2,1)} async-done(((bf16[128,768]{1,0:T(8,128)(2,1)}), bf16[4096,768]{1,0:T(8,128)(2,1)}) %all-gather.4.cloned.1.call-update) | async-done | bytes 6291472 | tf_op jit(solution)/shard_map/all_gather | solution.py:42
  246.6 71.8 %all-gather.6.cloned.1.call-done = bf16[4096,768]{1,0:T(8,128)(2,1)} async-done(((bf16[128,768]{1,0:T(8,128)(2,1)}), bf16[4096,768]{1,0:T(8,128)(2,1)}) %all-gather.6.cloned.1.call-update) | async-done | bytes 6291472 | tf_op jit(solution)/shard_map/all_gather | solution.py:43
  318.3 129.0 %while.18 = (s32[]{:T(128)}, f32[32,128]{1,0:T(8,128)S(1)}, f32[32,128]{1,0:T(8,128)}, f32[32,128,24]{1,2,0:T(8,128)S(1)}, bf16[4096,768]{1,0:T(8,128)(2,1)}, /*...) while((s32[]{:T(128)}, f32[32,128]{1,0:T(8,128)S(1)}, ...), condition=%wide.region_4.0_spmd.clone, body=%wide.region_1.0_spmd.clone.sunk | while | flops 618983424 | bytes 55515500 | solution.py:78
  319.0 2.7 constant_dynamic-slice_fusion.3
  321.6 1.4 copy.43
  323.0 2.4 copy.44
  325.4 4.5 fusion.46
  329.9 1.8 fusion.47
  331.8 1.3 fusion.48
  333.1 1.2 fusion.50
  335.1 2.7 constant_dynamic-slice_fusion.3
  337.8 1.4 copy.43
  339.2 2.4 copy.44
  341.5 4.5 fusion.46
  346.1 1.8 fusion.47
  347.9 1.3 fusion.48
  351.2 2.7 constant_dynamic-slice_fusion.3
  353.9 1.4 copy.43
  355.3 2.4 copy.44
  357.7 4.5 fusion.46
  362.2 1.8 fusion.47
  364.1 1.3 fusion.48
  367.4 2.7 constant_dynamic-slice_fusion.3
  370.0 1.4 copy.43
  371.4 2.4 copy.44
  373.8 4.5 fusion.46
  378.3 1.8 fusion.47
  380.2 1.3 fusion.48
  381.5 1.2 fusion.50
  383.5 2.7 constant_dynamic-slice_fusion.3
  386.1 1.4 copy.43
  387.5 2.4 copy.44
  389.9 4.5 fusion.46
  394.4 1.8 fusion.47
  396.3 1.3 fusion.48
  399.6 2.7 constant_dynamic-slice_fusion.3
  402.3 1.4 copy.43
  403.7 2.4 copy.44
  406.0 4.5 fusion.46
  410.6 1.8 fusion.47
  412.4 1.3 fusion.48
  415.7 2.7 constant_dynamic-slice_fusion.3
  418.4 1.4 copy.43
  419.8 2.4 copy.44
  422.2 4.5 fusion.46
  426.7 1.8 fusion.47
  428.6 1.3 fusion.48
  429.9 1.2 fusion.50
  431.8 2.7 constant_dynamic-slice_fusion.3
  434.5 1.4 copy.43
  435.9 2.4 copy.44
  438.3 4.5 fusion.46
  442.8 1.8 fusion.47
  444.7 1.3 fusion.48
  446.0 1.2 fusion.50
  (163 shorter events, 14.5 us)
Async XLA Ops:
  6.5 168.3 %copy-start = (bf16[768,1536]{1,0:T(8,128)(2,1)S(1)}, bf16[768,1536]{1,0:T(8,128)(2,1)}, u32[]{:S(2)}) copy-start(bf16[768,1536]{1,0:T(8,128)(2,1)} %param.15) | copy-start | bytes 7077892
  6.5 22.3 %copy-start.11 = (s32[1,8]{1,0:T(1,128)S(1)}, s32[1,8]{1,0:T(1,128)}, u32[]{:S(2)}) copy-start(s32[1,8]{1,0:T(1,128)} %param.12) | copy-start | bytes 100
  9.6 163.3 %copy-start.3 = (bf16[128,768]{1,0:T(8,128)(2,1)S(1)}, bf16[128,768]{1,0:T(8,128)(2,1)}, u32[]{:S(2)}) copy-start(bf16[128,768]{1,0:T(8,128)(2,1)} %param.10) | copy-start | bytes 589828
  9.6 163.3 %copy-start.6 = (bf16[128,1024]{1,0:T(8,128)(2,1)S(1)}, bf16[128,1024]{1,0:T(8,128)(2,1)}, u32[]{:S(2)}) copy-start(bf16[128,1024]{1,0:T(8,128)(2,1)} %param.11) | copy-start | bytes 786436
  9.6 159.6 %all-to-all-start = ((bf16[16,128,768]{2,1,0:T(8,128)(2,1)}), bf16[16,128,768]{2,1,0:T(8,128)(2,1)}, u32[]{:S(2)}, u32[]{:S(2)}) async-start(bf16[16,128,768]{2,1,0:T(8,128)(2,1)} %stack.2), calls=%async_computation | async-start | bytes 6291456 | tf_op jit(solution)/shard_map/all_to_all | solution.py:20
  28.2 218.4 %all-gather.4.cloned.1.call-start = ((), (), s32[]{:S(2)}) async-start(), calls=%async_computation.1 | async-start | bytes 6488064 | tf_op jit(solution)/shard_map/all_gather | solution.py:42
  172.9 5.6 %copy-start.9 = (f32[32,256]{1,0:T(8,128)S(1)}, f32[32,256]{1,0:T(8,128)}, u32[]{:S(2)}) copy-start(f32[32,256]{1,0:T(8,128)} %param.17) | copy-start | bytes 98308
  172.9 5.7 %copy-start.10 = (s32[128]{0:T(128)S(1)}, s32[128]{0:T(128)}, u32[]{:S(2)}) copy-start(s32[128]{0:T(128)} %param.14) | copy-start | bytes 1540
  176.1 142.2 %all-gather.6.cloned.1.call-start = ((), (), s32[]{:S(2)}) async-start(), calls=%async_computation.2 | async-start | bytes 6488064 | tf_op jit(solution)/shard_map/all_gather | solution.py:43
  318.3 3.3 copy-start.7
  325.4 4.5 copy-start.2
  331.8 1.3 copy-start.4
  331.8 1.3 copy-start.1
  333.1 1.3 copy-start.5
  333.1 1.3 copy-start.8
  334.4 3.3 copy-start.7
  341.5 4.5 copy-start.2
  347.9 1.3 copy-start.4
  347.9 1.3 copy-start.1
  349.2 1.3 copy-start.5
  349.3 1.3 copy-start.8
  350.5 3.3 copy-start.7
  357.7 4.5 copy-start.2
  364.0 1.3 copy-start.4
  364.1 1.3 copy-start.1
  365.4 1.3 copy-start.5
  365.4 1.3 copy-start.8
  366.7 3.3 copy-start.7
  373.8 4.5 copy-start.2
  380.2 1.3 copy-start.4
  380.2 1.3 copy-start.1
  381.5 1.3 copy-start.5
  381.5 1.3 copy-start.8
  382.8 3.3 copy-start.7
  389.9 4.5 copy-start.2
  396.3 1.3 copy-start.4
  396.3 1.3 copy-start.1
  397.6 1.3 copy-start.5
  397.6 1.3 copy-start.8
  398.9 3.3 copy-start.7
  406.0 4.5 copy-start.2
  412.4 1.3 copy-start.4
  412.4 1.3 copy-start.1
  413.7 1.3 copy-start.5
  413.8 1.3 copy-start.8
  415.0 3.3 copy-start.7
  422.2 4.5 copy-start.2
  428.5 1.3 copy-start.4
  428.6 1.3 copy-start.1
  429.9 1.3 copy-start.5
  429.9 1.3 copy-start.8
  431.2 3.3 copy-start.7
  438.3 4.5 copy-start.2
  444.7 1.3 copy-start.4
  444.7 1.3 copy-start.1
  446.0 1.3 copy-start.5
  446.0 1.3 copy-start.8
Sparse Core Ops, SparseCore 0:
  176.2 70.2 all-gather.3
  248.7 69.5 all-gather.5
